TPU v7x, 512 devices: a whole 4x4x16 slice. The times are simulated.
512 devices in a mesh: samp: 32 (over y_hi, z), head: 16 (over y_lo, x, core).
Axes of the slice: x: 4, y: 4 (y_hi: 2, y_lo: 2; y = y_hi * 2 + y_lo), z: 16, core: 2. Of those that a mesh axis runs over, the one named last changes fastest.
Arguments:
- queries: bfloat16 [32, 768, 512], P('samp', 'head'), may hold values from -10 to 10
- keys: bfloat16 [32, 768, 512], P('samp', 'head'), may hold values from -10 to 10
- values: bfloat16 [32, 768, 512], P('samp', 'head'), may hold values from -6 to 6
- out_grad: bfloat16 [32, 768, 512], P('samp', 'head'), may hold values from -6 to 6
- pair: bfloat16 [512, 512, 128], P('head', 'samp'), may hold values from -6 to 6
- ln_gain: float32 [128], replicated, may hold values from 0.25 to 1.75
- proj_weight: bfloat16 [128, 16], replicated, may hold values from -0.5 to 0.5
- token_mask: int32 [512], replicated, may hold values from 0 to 1, as said below
- atom_map: int32 [4096], replicated, may hold values from 0 to 511, never falling along the last dimension, each value on 1 to 24 neighbouring positions
Outputs:
- attended: bfloat16 [32, 768, 512], P('samp', 'head')
- query_grad: bfloat16 [32, 768, 512], P('samp', 'head')
- key_grad: bfloat16 [32, 768, 512], P('samp', 'head')
- value_grad: bfloat16 [32, 768, 512], P('samp', 'head')
- pair_grad: bfloat16 [512, 512, 128], P('head', 'samp')
- weight_grad: float32 [128, 16], replicated
- gain_grad: float32 [128], replicated
Inputs may be any that keep to these rules, and one draw needn't show every extreme that they name: `token_mask`: real tokens form a prefix of 256 or more tokens; the last token is padding.
All inputs are finite; a program needn't handle non-finite values.
Results may differ from a plain program's by a relative error of at most 0.02.
Values may be sent and summed in bfloat16 or wider, within the bound.
A program may use at most 64 MiB of HBM per device.

v0:
```python
import jax
import jax.numpy as jnp
from jax import lax
from jax.sharding import PartitionSpec as P


def token_weights(atom_map, token_mask):
    count = token_mask.shape[0]
    ends = jnp.searchsorted(atom_map, jnp.arange(count, dtype=jnp.int32), side="right")
    starts = jnp.concatenate([jnp.zeros((1,), jnp.int32), ends[:-1]])
    return (
        (ends - starts).astype(jnp.float32)
        * (count / atom_map.shape[0])
        * token_mask.astype(jnp.float32)
    )


def attend(query_row, key_row, value_row, grad_row, bias, key_keep, tok_weight):
    count = query_row.shape[1]
    local_heads = bias.shape[0]
    query_h = query_row.reshape(local_heads, -1, count)
    key_h = key_row.reshape(local_heads, -1, count)
    value_h = value_row.reshape(local_heads, -1, count)
    inv_root = 1.0 / jnp.sqrt(jnp.float32(query_h.shape[1]))
    scores = jnp.einsum(
        "hdi,hdj->hij", query_h, key_h, preferred_element_type=jnp.float32
    ) * inv_root + bias.astype(jnp.float32)
    scores = jnp.where(key_keep[None, None, :], scores, jnp.float32(-1000000000.0))
    largest = jnp.max(scores, axis=-1, keepdims=True)
    expo = jnp.exp(scores - largest)
    prob = expo / jnp.sum(expo, axis=-1, keepdims=True)
    prob_b = prob.astype(jnp.bfloat16)
    attended = jnp.einsum(
        "hij,hdj->hdi", prob_b, value_h, preferred_element_type=jnp.float32
    ).astype(jnp.bfloat16)
    grad_in = (grad_row.astype(jnp.float32) * tok_weight[None, :]).astype(jnp.bfloat16)
    grad_h = grad_in.reshape(local_heads, -1, count)
    dprob = jnp.einsum("hdi,hdj->hij", grad_h, value_h, preferred_element_type=jnp.float32)
    row_dot = jnp.sum(prob * dprob, axis=-1, keepdims=True)
    dscore = prob * (dprob - row_dot)
    dscore_b = dscore.astype(jnp.bfloat16)
    query_grad = (
        jnp.einsum("hij,hdj->hdi", dscore_b, key_h, preferred_element_type=jnp.float32) * inv_root
    ).astype(jnp.bfloat16)
    key_grad = (
        jnp.einsum("hij,hdi->hdj", dscore_b, query_h, preferred_element_type=jnp.float32) * inv_root
    ).astype(jnp.bfloat16)
    value_grad = jnp.einsum(
        "hij,hdi->hdj", prob_b, grad_h, preferred_element_type=jnp.float32
    ).astype(jnp.bfloat16)
    shape = (-1, count)
    return (
        attended.reshape(shape),
        query_grad.reshape(shape),
        key_grad.reshape(shape),
        value_grad.reshape(shape),
        dscore,
    )


def local(queries, keys, values, out_grad, pair, ln_gain, proj_weight, token_mask, atom_map):
    count = queries.shape[2]
    key_keep = token_mask > 0
    tok_weight = token_weights(atom_map, token_mask)
    wide = pair.astype(jnp.float32)
    center = jnp.mean(wide, axis=-1, keepdims=True)
    spread = jnp.mean(jnp.square(wide - center), axis=-1, keepdims=True)
    inv_std = 1.0 / jnp.sqrt(spread + 1e-05)
    normed = (wide - center) * inv_std
    lnout = (normed * ln_gain).astype(jnp.bfloat16)
    tile_bias = jnp.einsum(
        "ijc,ch->hij", lnout, proj_weight, preferred_element_type=jnp.float32
    ).astype(jnp.bfloat16)
    wide_rows = lax.all_gather(tile_bias, "samp", axis=2, tiled=True)
    bias = lax.all_to_all(wide_rows, "head", split_axis=0, concat_axis=1, tiled=True)

    def one_sample(total, items):
        query_row, key_row, value_row, grad_row = items
        attended, query_grad, key_grad, value_grad, dscore = attend(
            query_row, key_row, value_row, grad_row, bias, key_keep, tok_weight
        )
        return (total + dscore, (attended, query_grad, key_grad, value_grad))

    start = jnp.zeros(bias.shape, jnp.float32)
    bias_partial, outs = lax.scan(one_sample, start, (queries, keys, values, out_grad))
    attended, query_grad, key_grad, value_grad = outs
    summed = lax.psum_scatter(
        bias_partial.astype(jnp.bfloat16), "samp", scatter_dimension=2, tiled=True
    ).astype(jnp.float32)
    bias_grad = lax.all_to_all(
        summed.astype(jnp.bfloat16), "head", split_axis=1, concat_axis=0, tiled=True
    ).astype(summed.dtype)
    highest = lax.Precision.HIGHEST
    lnout_grad = jnp.einsum(
        "hij,ch->ijc", bias_grad, proj_weight.astype(jnp.float32), precision=highest
    )
    weight_part = jnp.einsum("ijc,hij->ch", lnout.astype(jnp.float32), bias_grad, precision=highest)
    gain_part = jnp.sum(lnout_grad * normed, axis=(0, 1))
    weight_sum, gain_sum = lax.psum((weight_part, gain_part), ("samp", "head"))
    scaled = lnout_grad * ln_gain
    pair_grad = (
        scaled
        - jnp.mean(scaled, axis=-1, keepdims=True)
        - normed * jnp.mean(scaled * normed, axis=-1, keepdims=True)
    ) * inv_std
    return (
        attended,
        query_grad,
        key_grad,
        value_grad,
        pair_grad.astype(jnp.bfloat16),
        weight_sum / count,
        gain_sum / count,
    )


def solution(mesh):
    placed = (
        P("samp", "head", None),
        P("samp", "head", None),
        P("samp", "head", None),
        P("samp", "head", None),
        P("head", "samp", None),
        P(),
        P(),
        P(),
        P(),
    )
    return jax.shard_map(
        local,
        mesh=mesh,
        in_specs=placed,
        out_specs=(
            P("samp", "head", None),
            P("samp", "head", None),
            P("samp", "head", None),
            P("samp", "head", None),
            P("head", "samp", None),
            P(),
            P(),
        ),
        check_vma=False,
    )
```

profile of v0, /device:TPU:1, one launch (start us, length us, event | category | flops | bytes accessed | tf_op | source)
XLA Modules:
  0.0 939.2 jit_solution(5410960035745740067)
XLA Ops:
  7.2 1.1 convert_reduce_fusion
  8.3 1.1 fusion.25
  9.4 1.2 fusion.4
  10.7 104.2 %all_gather.3 = bf16[16,32,512]{0,2,1:T(8,128)(2,1)} all-gather(bf16[16,32,16]{0,2,1:T(8,128)(2,1)S(1)} %fusion.4), channel_id=1, replica_groups=mesh['samp'=32,'head'=16] {'samp'}, dimensions={2}, use_global_device_ids=true | all-gather | bytes 540672 | tf_op jit(solution)/shard_map/all_gather | solution.py:74
  114.9 4.6 copy.27
  119.5 17.6 %all-to-all-start = ((bf16[16,32,512]{2,1,0:T(8,128)(2,1)}), bf16[16,32,512]{2,1,0:T(8,128)(2,1)S(1)}, u32[]{:S(2)}, u32[]{:S(2)}) async-start(bf16[16,32,512]{2,1,0:T(8,128)(2,1)} %copy.27), calls=%async_computation | async-start | bytes 1048576 | tf_op jit(solution)/shard_map/all_to_all | solution.py:75
  137.2 42.1 %while.32 = (s32[]{:T(128)}, u32[512]{0:T(512)S(1)}, u32[512]{0:T(512)S(1)}, s32[4096]{0:T(1024)S(1)}, s32[]{:T(128)}, /*index=5*/s32[]{:T(128)}, s32[]{}) while((s32[]{:T(128)}, u32[512]{0:T(512)S(1)}, u32[512]{0:T(512)S(1)}, s32[4096]{0:T(1024)S(1)}, s32[]{:T(128)}, /*index=5*/s32[]{:T(128)}, s32[]{}) %tuple.50), condition=%wide.region_5.6_spmd.clone, body=%wide.region_4.5_spmd.clone.sunk | while | flops 10244 | bytes 37989 | solution.py:9
  137.2 3.1 gather_fusion
  140.5 3.1 gather_fusion
  143.7 3.1 gather_fusion
  146.9 3.1 gather_fusion
  150.2 3.1 gather_fusion
  153.4 3.1 gather_fusion
  156.6 3.1 gather_fusion
  159.9 3.1 gather_fusion
  163.1 3.1 gather_fusion
  166.4 3.1 gather_fusion
  169.6 3.1 gather_fusion
  172.8 3.1 gather_fusion
  176.1 3.1 gather_fusion
  179.3 0.1 fusion.51
  179.4 0.1 bitcast_convert_fusion
  179.6 0.3 copy.28
  179.9 0.4 fusion.54
  180.3 0.2 fusion.12
  180.5 0.4 multiply_reduce_fusion
  180.9 1.1 multiply_convert_fusion
  182.0 1.9 fusion.7
  183.9 0.9 fusion.10
  184.8 0.9 fusion.9
  185.7 616.3 %reduce-scatter.2.cloned.1.call-done = bf16[1,512,16]{1,2,0:T(8,128)(2,1)} async-done(((bf16[1,512,512]{1,2,0:T(8,128)(2,1)}), bf16[1,512,16]{1,2,0:T(8,128)(2,1)}) %reduce-scatter.2.cloned.1.call-update) | async-done | bytes 16400 | tf_op jit(solution)/shard_map/reduce_scatter | solution.py:87
  802.0 0.9 copy.29
  802.9 0.5 broadcast.127
  803.4 1.4 reduce.6
  804.9 0.8 reshape.193
  805.6 16.4 %all-to-all-start.1 = ((bf16[16,2,256]{2,1,0:T(2,128)(2,1)}), bf16[16,2,256]{2,1,0:T(2,128)(2,1)S(1)}, u32[]{:S(2)}, u32[]{:S(2)}) async-start(bf16[16,2,256]{2,1,0:T(2,128)(2,1)} %reshape.193), calls=%async_computation.2 | async-start | bytes 32768 | tf_op jit(solution)/shard_map/all_to_all | solution.py:90
  822.0 0.9 fusion.8
  822.9 4.9 all-to-all-done.1
  827.8 0.2 reshape.194
  828.0 0.1 copy.30
  828.1 0.1 all_to_all.8
  828.2 0.2 copy.32
  828.4 0.4 fusion.24
  828.9 0.3 convolution_bitcast_fusion
  829.2 101.0 %all-reduce = (f32[128,16]{0,1:T(8,128)S(1)}, f32[128]{0:T(128)S(1)}) all-reduce(f32[128,16]{0,1:T(8,128)S(1)} %convolution_bitcast_fusion, f32[128]{0:T(128)S(1)} %get-tuple-element.129), channel_id=1, replica_groups=mesh['samp'=32,'head'=16] {'samp','head'}, use_global_device_ids=true, to_apply=%region_10.11 | all-reduce | flops 2176 | bytes 17408 | tf_op jit(solution)/shard_map/psum | solution.py:99
  930.2 0.6 broadcast_multiply_fusion.3
  930.8 0.5 broadcast_multiply_fusion.4
  931.3 1.0 fusion.23
  (95 shorter events, 0.7 us)
Async XLA Ops:
  7.2 172.8 %copy-start = (bf16[1,48,512]{2,1,0:T(8,128)(2,1)S(1)}, bf16[1,48,512]{2,1,0:T(8,128)(2,1)}, u32[]{:S(2)}) copy-start(bf16[1,48,512]{2,1,0:T(8,128)(2,1)} %param.12) | copy-start | bytes 147460
  10.7 126.5 %copy-start.1 = (s32[4096]{0:T(1024)S(1)}, s32[4096]{0:T(1024)}, u32[]{:S(2)}) copy-start(s32[4096]{0:T(1024)} %param.19) | copy-start | bytes 49156
  119.5 59.9 %all-to-all-start = ((bf16[16,32,512]{2,1,0:T(8,128)(2,1)}), bf16[16,32,512]{2,1,0:T(8,128)(2,1)S(1)}, u32[]{:S(2)}, u32[]{:S(2)}) async-start(bf16[16,32,512]{2,1,0:T(8,128)(2,1)} %copy.27), calls=%async_computation | async-start | bytes 1048576 | tf_op jit(solution)/shard_map/all_to_all | solution.py:75
  137.1 664.9 %reduce-scatter.2.cloned.1.call-start = ((), (), s32[]{:S(2)}) async-start(), calls=%async_computation.3 | async-start | bytes 540672 | tf_op jit(solution)/shard_map/reduce_scatter | solution.py:87
  137.2 42.2 %copy-start.5 = (s32[512]{0:T(512)S(1)}, s32[512]{0:T(512)}, u32[]{:S(2)}) copy-start(s32[512]{0:T(512)} %param.18) | copy-start | bytes 6148
  137.2 42.8 %copy-start.4 = (bf16[1,48,512]{2,1,0:T(8,128)(2,1)S(1)}, bf16[1,48,512]{2,1,0:T(8,128)(2,1)}, u32[]{:S(2)}) copy-start(bf16[1,48,512]{2,1,0:T(8,128)(2,1)} %param.11) | copy-start | bytes 147460
  179.3 1.2 copy-start.7
  179.3 1.2 copy-start.8
  183.9 638.1 %copy-start.2 = (bf16[512,512]{0,1:T(8,128)(2,1)S(1)}, bf16[512,512]{0,1:T(8,128)(2,1)}, u32[]{:S(2)}) copy-start(bf16[512,512]{0,1:T(8,128)(2,1)} %multiply_convert_fusion) | copy-start | bytes 1572868
  184.8 643.6 %copy-start.3 = (bf16[32,16,128]{2,1,0:T(8,128)(2,1)S(1)}, bf16[32,16,128]{2,1,0:T(8,128)(2,1)}, u32[]{:S(2)}) copy-start(bf16[32,16,128]{2,1,0:T(8,128)(2,1)} %param.15) | copy-start | bytes 393220
  184.8 643.6 %copy-start.6 = (f32[128]{0:T(128)S(1)}, f32[128]{0:T(128)}, u32[]{:S(2)}) copy-start(f32[128]{0:T(128)} %param.16) | copy-start | bytes 1540
  184.8 643.6 %copy-start.9 = (bf16[128,16]{0,1:T(8,128)(2,1)S(1)}, bf16[128,16]{0,1:T(8,128)(2,1)}, u32[]{:S(2)}) copy-start(bf16[128,16]{0,1:T(8,128)(2,1)} %param.17) | copy-start | bytes 12292
  805.6 22.2 %all-to-all-start.1 = ((bf16[16,2,256]{2,1,0:T(2,128)(2,1)}), bf16[16,2,256]{2,1,0:T(2,128)(2,1)S(1)}, u32[]{:S(2)}, u32[]{:S(2)}) async-start(bf16[16,2,256]{2,1,0:T(2,128)(2,1)} %reshape.193), calls=%async_computation.2 | async-start | bytes 32768 | tf_op jit(solution)/shard_map/all_to_all | solution.py:90
Sparse Core Ops, SparseCore 0:
  182.1 619.8 reduce-scatter.1
where the time goes:
time: 940 us; the launch traced here: 939 us
  waiting for transfers between devices  621 us (66%)
  blocking collectives  205 us (22%)
  local copies, waits for them, and re-layouts  48.6 us (5%)
  starting transfers between devices  34 us (4%)
  between operations  14.3 us (2%)
    reduce_scatter x1, waiting for transfers between devices, local(): lax.psum_scatter(bias_partial.astype(jnp.bfloat16), 'samp', scatter_dimen...  616 us
    all_gather x1, blocking collectives, local(): wide_rows = lax.all_gather(tile_bias, 'samp', axis=2, tiled=True)  104 us
    psum x1, blocking collectives, local(): weight_sum, gain_sum = lax.psum((weight_part, gain_part), ('samp', 'head'))  101 us
    gather x13, local copies, waits for them, and re-layouts, token_weights(): jnp.searchsorted(atom_map, jnp.arange(count, dtype=jnp.int32), side='right')  40.9 us
  transfers between devices with their start and end apart: 3, of which 2 were waited for; matrix products, arithmetic and copies ran while one was open for 5% of the time, Pallas kernels for 0%

commit v1 on v0

--- a/solution.py
+++ b/solution.py
@@ -2,6 +2,11 @@
 import jax.numpy as jnp
 from jax import lax
 from jax.sharding import PartitionSpec as P
+
+
+def swapped_in(x, axis, along):
+    stack = jnp.stack([x] * lax.axis_size(axis))
+    return jnp.concatenate(lax.all_to_all(stack, axis, 0, 0), axis=along)
 
 
 def token_weights(atom_map, token_mask):
@@ -71,7 +76,7 @@
     tile_bias = jnp.einsum(
         "ijc,ch->hij", lnout, proj_weight, preferred_element_type=jnp.float32
     ).astype(jnp.bfloat16)
-    wide_rows = lax.all_gather(tile_bias, "samp", axis=2, tiled=True)
+    wide_rows = swapped_in(tile_bias, "samp", 2)
     bias = lax.all_to_all(wide_rows, "head", split_axis=0, concat_axis=1, tiled=True)
 
     def one_sample(total, items):

time: 940 us -> 880 us (0.936)
  blocking collectives: 205 us -> 101 us
  waiting for transfers between devices: 621 us -> 656 us
    all_gather x1 -> x0, blocking collectives: 104 us -> none  [local(): wide_rows = lax.all_gather(tile_bias, 'samp', axis=2, tiled=True)]
    all_to_all x0 -> x1, waiting for transfers between devices: none -> 32.1 us  [swapped_in(): return jnp.concatenate(lax.all_to_all(stack, axis, 0, 0), axis=along)]
    all_to_all x0 -> x1, starting transfers between devices: none -> 18.6 us  [swapped_in(): return jnp.concatenate(lax.all_to_all(stack, axis, 0, 0), axis=along)]
    all_to_all x1, starting transfers between devices: 17.6 us -> 5.91 us  [local(): lax.all_to_all(wide_rows, 'head', split_axis=0, concat_axis=1, tiled=True)]
  transfers between devices with their start and end apart: 3 -> 4, of which waited for: 2 -> 3; matrix products, arithmetic and copies ran while one was open for 5% -> 5% of each run, Pallas kernels for 0% -> 0%
where the time goes in v1:
time: 880 us; the launch traced here: 879 us
  waiting for transfers between devices  656 us (75%)
  blocking collectives  101 us (11%)
  local copies, waits for them, and re-layouts  51.2 us (6%)
  starting transfers between devices  40.9 us (5%)
  between operations  14.3 us (2%)
    reduce_scatter x1, waiting for transfers between devices, local(): lax.psum_scatter(bias_partial.astype(jnp.bfloat16), 'samp', scatter_dimen...  619 us
    psum x1, blocking collectives, local(): weight_sum, gain_sum = lax.psum((weight_part, gain_part), ('samp', 'head'))  101 us
    gather x13, local copies, waits for them, and re-layouts, token_weights(): jnp.searchsorted(atom_map, jnp.arange(count, dtype=jnp.int32), side='right')  40.9 us
    all_to_all x1, waiting for transfers between devices, swapped_in(): return jnp.concatenate(lax.all_to_all(stack, axis, 0, 0), axis=along)  32.1 us
    all_to_all x1, starting transfers between devices, swapped_in(): return jnp.concatenate(lax.all_to_all(stack, axis, 0, 0), axis=along)  18.6 us
  transfers between devices with their start and end apart: 4, of which 3 were waited for; matrix products, arithmetic and copies ran while one was open for 5% of the time, Pallas kernels for 0%

profile of v1, /device:TPU:1, one launch (start us, length us, event | category | flops | bytes accessed | tf_op | source)
XLA Modules:
  0.0 879.4 jit_solution(7339745270536019750)
XLA Ops:
  7.2 1.1 convert_reduce_fusion
  8.3 1.1 fusion.25
  9.4 1.2 fusion.4
  10.9 0.5 broadcast_bitcast_fusion
  11.3 2.7 reshape.203
  14.1 18.6 %all-to-all-start = ((bf16[32,2,4096]{2,1,0:T(2,128)(2,1)}), bf16[32,2,4096]{2,1,0:T(2,128)(2,1)S(1)}, u32[]{:S(2)}, u32[]{:S(2)}) async-start(bf16[32,2,4096]{2,1,0:T(2,128)(2,1)} %reshape.203), calls=%async_computation | async-start | bytes 1048576 | tf_op jit(solution)/shard_map/all_to_all | solution.py:9
  32.7 32.1 %all-to-all-done = bf16[32,2,4096]{2,1,0:T(2,128)(2,1)S(1)} async-done(((bf16[32,2,4096]{2,1,0:T(2,128)(2,1)}), bf16[32,2,4096]{2,1,0:T(2,128)(2,1)S(1)}, u32[]{:S(2)}, u32[]{:S(2)}) %all-to-all-start) | async-done | bytes 524320 | tf_op jit(solution)/shard_map/all_to_all | solution.py:9
  64.9 1.0 reshape.204
  65.9 0.4 bitcast_bitcast_fusion
  66.3 0.5 copy.35
  66.8 1.5 copy.36
  68.3 5.9 all-to-all-start.1
  74.3 42.1 %while.32 = (s32[]{:T(128)}, u32[512]{0:T(512)S(1)}, u32[512]{0:T(512)S(1)}, s32[4096]{0:T(1024)S(1)}, s32[]{:T(128)}, /*index=5*/s32[]{:T(128)}, s32[]{}) while((s32[]{:T(128)}, u32[512]{0:T(512)S(1)}, u32[512]{0:T(512)S(1)}, s32[4096]{0:T(1024)S(1)}, s32[]{:T(128)}, /*index=5*/s32[]{:T(128)}, s32[]{}) %tuple.50), condition=%wide.region_5.6_spmd.clone, body=%wide.region_4.5_spmd.clone.sunk | while | flops 10244 | bytes 37989 | solution.py:14
  74.3 3.1 gather_fusion
  77.6 3.1 gather_fusion
  80.8 3.1 gather_fusion
  84.1 3.1 gather_fusion
  87.3 3.1 gather_fusion
  90.5 3.1 gather_fusion
  93.8 3.1 gather_fusion
  97.0 3.1 gather_fusion
  100.3 3.1 gather_fusion
  103.5 3.1 gather_fusion
  106.7 3.1 gather_fusion
  110.0 3.1 gather_fusion
  113.2 3.1 gather_fusion
  116.7 0.3 copy.37
  117.2 0.4 fusion.54
  118.0 0.4 multiply_reduce_fusion
  118.4 1.1 multiply_convert_fusion
  119.5 1.9 fusion.7
  121.4 0.9 fusion.10
  122.3 0.9 fusion.9
  123.2 619.0 %reduce-scatter.2.cloned.1.call-done = bf16[1,512,16]{1,2,0:T(8,128)(2,1)} async-done(((bf16[1,512,512]{1,2,0:T(8,128)(2,1)}), bf16[1,512,16]{1,2,0:T(8,128)(2,1)}) %reduce-scatter.2.cloned.1.call-update) | async-done | bytes 16400 | tf_op jit(solution)/shard_map/reduce_scatter | solution.py:92
  742.2 0.9 copy.38
  743.1 0.5 broadcast.129
  743.6 1.5 reduce.6
  745.1 0.8 reshape.205
  745.9 16.3 %all-to-all-start.2 = ((bf16[16,2,256]{2,1,0:T(2,128)(2,1)}), bf16[16,2,256]{2,1,0:T(2,128)(2,1)S(1)}, u32[]{:S(2)}, u32[]{:S(2)}) async-start(bf16[16,2,256]{2,1,0:T(2,128)(2,1)} %reshape.205), calls=%async_computation.3 | async-start | bytes 32768 | tf_op jit(solution)/shard_map/all_to_all | solution.py:95
  762.2 0.9 fusion.8
  763.1 4.9 all-to-all-done.2
  768.0 0.2 reshape.206
  768.6 0.4 fusion.24
  769.1 0.3 convolution_bitcast_fusion
  769.4 101.1 %all-reduce = (f32[128,16]{0,1:T(8,128)S(1)}, f32[128]{0:T(128)S(1)}) all-reduce(f32[128,16]{0,1:T(8,128)S(1)} %convolution_bitcast_fusion, f32[128]{0:T(128)S(1)} %get-tuple-element.129), channel_id=1, replica_groups=mesh['samp'=32,'head'=16] {'samp','head'}, use_global_device_ids=true, to_apply=%region_10.11 | all-reduce | flops 2176 | bytes 17408 | tf_op jit(solution)/shard_map/psum | solution.py:104
  870.5 0.6 broadcast_multiply_fusion.3
  871.1 0.5 broadcast_multiply_fusion.4
  871.6 1.0 fusion.23
  (102 shorter events, 2.1 us)
Async XLA Ops:
  7.2 109.9 %copy-start = (bf16[1,48,512]{2,1,0:T(8,128)(2,1)S(1)}, bf16[1,48,512]{2,1,0:T(8,128)(2,1)}, u32[]{:S(2)}) copy-start(bf16[1,48,512]{2,1,0:T(8,128)(2,1)} %param.12) | copy-start | bytes 147460
  14.1 50.8 %all-to-all-start = ((bf16[32,2,4096]{2,1,0:T(2,128)(2,1)}), bf16[32,2,4096]{2,1,0:T(2,128)(2,1)S(1)}, u32[]{:S(2)}, u32[]{:S(2)}) async-start(bf16[32,2,4096]{2,1,0:T(2,128)(2,1)} %reshape.203), calls=%async_computation | async-start | bytes 1048576 | tf_op jit(solution)/shard_map/all_to_all | solution.py:9
  66.8 7.5 copy-start.1
  68.3 48.2 %all-to-all-start.1 = ((bf16[16,32,512]{2,1,0:T(8,128)(2,1)}), bf16[16,32,512]{2,1,0:T(8,128)(2,1)S(1)}, u32[]{:S(2)}, u32[]{:S(2)}) async-start(bf16[16,32,512]{2,1,0:T(8,128)(2,1)} %copy.36), calls=%async_computation.1 | async-start | bytes 1048576 | tf_op jit(solution)/shard_map/all_to_all | solution.py:80
  74.2 668.0 %reduce-scatter.2.cloned.1.call-start = ((), (), s32[]{:S(2)}) async-start(), calls=%async_computation.4 | async-start | bytes 540672 | tf_op jit(solution)/shard_map/reduce_scatter | solution.py:92
  74.3 42.1 %copy-start.5 = (s32[512]{0:T(512)S(1)}, s32[512]{0:T(512)}, u32[]{:S(2)}) copy-start(s32[512]{0:T(512)} %param.18) | copy-start | bytes 6148
  116.4 0.8 copy-start.4
  117.2 0.8 copy-start.7
  117.2 0.8 copy-start.8
  122.3 639.9 %copy-start.2 = (bf16[512,512]{0,1:T(8,128)(2,1)S(1)}, bf16[512,512]{0,1:T(8,128)(2,1)}, u32[]{:S(2)}) copy-start(bf16[512,512]{0,1:T(8,128)(2,1)} %multiply_convert_fusion) | copy-start | bytes 1572868
  123.2 645.4 %copy-start.3 = (bf16[32,16,128]{2,1,0:T(8,128)(2,1)S(1)}, bf16[32,16,128]{2,1,0:T(8,128)(2,1)}, u32[]{:S(2)}) copy-start(bf16[32,16,128]{2,1,0:T(8,128)(2,1)} %param.15) | copy-start | bytes 393220
  123.2 645.4 %copy-start.6 = (f32[128]{0:T(128)S(1)}, f32[128]{0:T(128)}, u32[]{:S(2)}) copy-start(f32[128]{0:T(128)} %param.16) | copy-start | bytes 1540
  123.2 645.4 %copy-start.9 = (bf16[128,16]{0,1:T(8,128)(2,1)S(1)}, bf16[128,16]{0,1:T(8,128)(2,1)}, u32[]{:S(2)}) copy-start(bf16[128,16]{0,1:T(8,128)(2,1)} %param.17) | copy-start | bytes 12292
  745.9 22.1 %all-to-all-start.2 = ((bf16[16,2,256]{2,1,0:T(2,128)(2,1)}), bf16[16,2,256]{2,1,0:T(2,128)(2,1)S(1)}, u32[]{:S(2)}, u32[]{:S(2)}) async-start(bf16[16,2,256]{2,1,0:T(2,128)(2,1)} %reshape.205), calls=%async_computation.3 | async-start | bytes 32768 | tf_op jit(solution)/shard_map/all_to_all | solution.py:95
Sparse Core Ops, SparseCore 0:
  119.6 622.5 reduce-scatter.1
